TPU v7x, 32 devices: a whole 2x2x4 slice. The times are simulated.
32 devices in a mesh: groups: 2 (over y), mem: 4 (over z), head: 2 (over x), width: 2 (over core).
Axes of the slice: x: 2, y: 2, z: 4, core: 2. Of those that a mesh axis runs over, the one named last changes fastest.
Arguments:
- residual_in: bfloat16 [64, 5120], P('groups', 'mem'), parts along dimension 0, may hold values from -26 to 26
- attention_gain: float32 [5120], P('mem'), may hold values from 0.5 to 1.5
- query_weight: bfloat16 [5120, 8192], P('mem', ('head', 'width')), may hold values from -0.078125 to 0.078125
- key_weight: bfloat16 [5120, 1024], P('mem', ('head', 'width')), may hold values from -0.078125 to 0.078125
- value_weight: bfloat16 [5120, 1024], P('mem', ('head', 'width')), may hold values from -0.078125 to 0.078125
- query_norm: float32 [128], replicated, may hold values from 0.25 to 1.75
- key_norm: float32 [128], replicated, may hold values from 0.1 to 1.9
- cache_keys: bfloat16 [65536, 8, 128], P(('groups', 'mem'), ('head', 'width')), parts along dimension 0, may hold values from -480 to 480
- cache_values: bfloat16 [65536, 8, 128], P(('groups', 'mem'), ('head', 'width')), parts along dimension 0, may hold values from -12 to 12
- slot_request: int32 [65536], P(('groups', 'mem')), parts along dimension 0, may hold values from 0 to 16, as said below
- lengths: int32 [32], P('groups'), parts along dimension 0, may hold values from 1056 to 1760, as said below
- output_weight: bfloat16 [8192, 5120], P(('head', 'width'), 'mem'), may hold values from -0.0625 to 0.0625
- second_gain: float32 [5120], P('mem'), may hold values from 0.5 to 1.5
- gate_weight: bfloat16 [5120, 25600], P('mem', ('head', 'width')), may hold values from -0.078125 to 0.078125
- up_weight: bfloat16 [5120, 25600], P('mem', ('head', 'width')), may hold values from -0.078125 to 0.078125
- down_weight: bfloat16 [25600, 5120], P(('head', 'width'), 'mem'), may hold values from -0.0390625 to 0.0390625
Outputs:
- layer_out: bfloat16 [64, 5120], P('groups', 'mem'), parts along dimension 0
There are 2 independent parts, one for each index of `groups`. A program takes and returns all parts, laid end to end along the dimension named above; an argument that names none is the same for every part. Nothing has to cross between parts.
Inputs may be any that keep to these rules, and one draw needn't show every extreme that they name: slot_request[s] names the request whose cached token sits in slot s, or is 16 for an empty slot. On each owner (each aligned block of 8192 slots along mem) the used slots come first; taking owners in order and their used slots in order, requests 0 to 15 follow one another in consecutive slots, so a request may continue on the next owner, but on no further one: a request's slots lie on at most two consecutive owners. Request r has exactly lengths[r] slots. Some owner has all its slots used. lengths[r] is the number of cached tokens of request r; its new tokens stand at positions lengths[r] and lengths[r] + 1.
All inputs are finite; a program needn't handle non-finite values.
Results may differ from a plain program's by a relative error of at most 0.0095.
The roundings to bfloat16 on the way count: a program that leaves them out, or rounds other values in their place, can miss the bound.
Values may be sent and summed in bfloat16 or wider, within the bound.
A program may use at most 128 MiB of HBM per device.

v0:
```python
import math
import jax
import jax.numpy as jnp
from jax import lax
from jax.sharding import PartitionSpec as P

D = 5120
epsilon = 1e-06
rope_base = 1000000.0
floor_score = -1e30


def combined_all(value, axis, join):
    pieces = jax.tree.map(lambda part: lax.all_gather(part, axis), value)
    head = jax.tree.map(lambda part: part[0], pieces)
    tail = jax.tree.map(lambda part: part[1:], pieces)
    running, _ = lax.scan(lambda running, slab: (join(running, slab), None), head, tail)
    return running


def rotate(values, places):
    breadth = values.shape[-1]
    halfway = breadth // 2
    frequency = rope_base ** (-(jnp.arange(halfway, dtype=jnp.float32) * 2.0) / breadth)
    angles = places[..., None] * frequency
    cosine = jnp.cos(angles)
    sine_part = jnp.sin(angles)
    leading = values[..., :halfway]
    trailing = values[..., halfway:]
    return jnp.concatenate(
        [leading * cosine - trailing * sine_part, trailing * cosine + leading * sine_part], axis=-1
    )


def head_norm(values, scaling):
    mean_square = jnp.mean(values * values, axis=-1, keepdims=True)
    return values * lax.rsqrt(mean_square + epsilon) * scaling


def combine(first, second):
    first_top, first_sum, first_acc = first
    second_top, second_sum, second_acc = second
    highest = jnp.maximum(first_top, second_top)
    first_factor = jnp.exp(first_top - highest)
    second_factor = jnp.exp(second_top - highest)
    return (
        highest,
        first_sum * first_factor + second_sum * second_factor,
        first_acc * first_factor[..., None] + second_acc * second_factor[..., None],
    )


def per_device(
    residual_in,
    attention_gain,
    query_weight,
    key_weight,
    value_weight,
    query_norm,
    key_norm,
    cache_keys,
    cache_values,
    slot_request,
    lengths,
    output_weight,
    second_gain,
    gate_weight,
    up_weight,
    down_weight,
):
    row_count = residual_in.shape[0]
    requests = row_count // 2
    head_dim = query_norm.shape[0]
    kv_here = cache_keys.shape[1]
    q_here = query_weight.shape[1] // head_dim
    group_size = q_here // kv_here
    score_scale = 1.0 / math.sqrt(head_dim)
    residual = residual_in.astype(jnp.float32)
    squares = lax.psum(jnp.sum(residual * residual, axis=1), "mem")
    normed = (residual * lax.rsqrt(squares / D + epsilon)[:, None] * attention_gain).astype(
        jnp.bfloat16
    )
    query_part = jnp.dot(normed, query_weight, preferred_element_type=jnp.float32)
    key_part = jnp.dot(normed, key_weight, preferred_element_type=jnp.float32)
    value_part = jnp.dot(normed, value_weight, preferred_element_type=jnp.float32)
    offsets = jnp.arange(2, dtype=jnp.int32)
    places = (lengths[:, None] + offsets[None, :]).reshape(row_count).astype(jnp.float32)
    query_sum, key_sum, value_sum = lax.psum((query_part, key_part, value_part), "mem")
    count_rows = query_sum.shape[0]
    query_rot = rotate(
        head_norm(query_sum.reshape(count_rows, q_here, head_dim), query_norm), places[:, None]
    )
    key_rot = rotate(
        head_norm(key_sum.reshape(count_rows, kv_here, head_dim), key_norm), places[:, None]
    )
    queries = query_rot.astype(jnp.bfloat16)
    new_keys = key_rot.astype(jnp.bfloat16)
    new_values = value_sum.reshape(count_rows, kv_here, head_dim).astype(jnp.bfloat16)
    queries_split = queries.reshape(row_count, kv_here, group_size, head_dim)
    row_owner = jnp.arange(row_count, dtype=jnp.int32) // 2
    capacity = cache_keys.shape[0]
    block_size = min(1024, capacity)
    used_slots = jnp.sum((slot_request < requests).astype(jnp.int32))
    used_blocks = (used_slots + block_size - 1) // block_size
    start_state = (
        jnp.full((row_count, kv_here, group_size), floor_score, jnp.float32),
        jnp.zeros((row_count, kv_here, group_size), jnp.float32),
        jnp.zeros((row_count, kv_here, group_size, head_dim), jnp.float32),
    )

    def visit_block(counter, carried):
        highest, summed, running = carried
        first_slot = counter * block_size
        key_block = lax.dynamic_slice_in_dim(cache_keys, first_slot, block_size, 0)
        value_block = lax.dynamic_slice_in_dim(cache_values, first_slot, block_size, 0)
        owner_block = lax.dynamic_slice_in_dim(slot_request, first_slot, block_size, 0)
        scores = (
            jnp.einsum(
                "bkgd,skd->bkgs", queries_split, key_block, preferred_element_type=jnp.float32
            )
            * score_scale
        )
        matches = (owner_block[None, :] == row_owner[:, None])[:, None, None, :]
        block_top = jnp.max(jnp.where(matches, scores, floor_score), axis=-1)
        updated = jnp.maximum(highest, block_top)
        weights = jnp.where(matches, jnp.exp(scores - updated[..., None]), 0.0)
        factor = jnp.exp(highest - updated)
        summed = summed * factor + jnp.sum(weights, axis=-1)
        running = running * factor[..., None] + jnp.einsum(
            "bkgs,skd->bkgd",
            weights.astype(jnp.bfloat16),
            value_block,
            preferred_element_type=jnp.float32,
        )
        return (updated, summed, running)

    highest, summed, running = lax.fori_loop(0, used_blocks, visit_block, start_state)
    highest, summed, running = combined_all((highest, summed, running), "mem", combine)
    query_pairs = queries.reshape(requests, 2, kv_here, group_size, head_dim)
    key_pairs = new_keys.reshape(requests, 2, kv_here, head_dim)
    value_pairs = new_values.reshape(requests, 2, kv_here, head_dim)
    allowed = (offsets[None, :] <= offsets[:, None])[None, :, None, None, :]
    allowed_rows = jnp.broadcast_to(allowed, (requests, 2, kv_here, group_size, 2)).reshape(
        row_count, kv_here, group_size, 2
    )
    own_scores = (
        jnp.einsum("rtkgd,rskd->rtkgs", query_pairs, key_pairs, preferred_element_type=jnp.float32)
        * score_scale
    )
    own_scores = jnp.where(allowed, own_scores, floor_score).reshape(
        row_count, kv_here, group_size, 2
    )
    final_top = jnp.maximum(highest, jnp.max(own_scores, axis=-1))
    own_weights = jnp.where(allowed_rows, jnp.exp(own_scores - final_top[..., None]), 0.0)
    factor = jnp.exp(highest - final_top)
    summed = summed * factor + jnp.sum(own_weights, axis=-1)
    own_rounded = own_weights.astype(jnp.bfloat16).reshape(requests, 2, kv_here, group_size, 2)
    own_values = jnp.einsum(
        "rtkgs,rskd->rtkgd", own_rounded, value_pairs, preferred_element_type=jnp.float32
    )
    running = running * factor[..., None] + own_values.reshape(
        row_count, kv_here, group_size, head_dim
    )
    attended = (
        (running / summed[..., None]).reshape(row_count, q_here * head_dim).astype(jnp.bfloat16)
    )
    projected = lax.psum(
        jnp.dot(attended, output_weight, preferred_element_type=jnp.float32), ("head", "width")
    )
    middle = (residual + projected).astype(jnp.bfloat16)
    middle_wide = middle.astype(jnp.float32)
    squares_mid = lax.psum(jnp.sum(middle_wide * middle_wide, axis=1), "mem")
    normed_mid = (middle_wide * lax.rsqrt(squares_mid / D + epsilon)[:, None] * second_gain).astype(
        jnp.bfloat16
    )
    gate_part = jnp.dot(normed_mid, gate_weight, preferred_element_type=jnp.float32)
    up_part = jnp.dot(normed_mid, up_weight, preferred_element_type=jnp.float32)
    gate_sum, up_sum = (
        lax.psum_scatter(gate_part, "mem", scatter_dimension=0, tiled=True),
        lax.psum_scatter(up_part, "mem", scatter_dimension=0, tiled=True),
    )
    activated = lax.all_gather(
        (jax.nn.silu(gate_sum) * up_sum).astype(jnp.bfloat16), "mem", axis=0, tiled=True
    )
    down_sum = lax.psum(
        jnp.dot(activated, down_weight, preferred_element_type=jnp.float32), ("head", "width")
    )
    return (middle_wide + down_sum).astype(jnp.bfloat16)


def solution(mesh):
    return jax.shard_map(
        per_device,
        mesh=mesh,
        in_specs=(
            P("groups", "mem"),
            P("mem"),
            P("mem", ("head", "width")),
            P("mem", ("head", "width")),
            P("mem", ("head", "width")),
            P(),
            P(),
            P(("groups", "mem"), ("head", "width"), None),
            P(("groups", "mem"), ("head", "width"), None),
            P(("groups", "mem")),
            P("groups"),
            P(("head", "width"), "mem"),
            P("mem"),
            P("mem", ("head", "width")),
            P("mem", ("head", "width")),
            P(("head", "width"), "mem"),
        ),
        out_specs=P("groups", "mem"),
        check_vma=False,
    )
```

profile of v0, /device:TPU:0, one launch (start us, length us, event | category | flops | bytes accessed | tf_op | source)
XLA Modules:
  0.0 318.0 jit_solution(10210930667824503828)
XLA Ops:
  7.7 13.5 %psum.49 = f32[32]{0:T(128)S(1)} all-reduce(f32[32]{0:T(128)S(1)} %fusion.24), channel_id=1, replica_groups=mesh['groups'=2,'mem'=4,'head'=2,'width'=2] {'mem'}, use_global_device_ids=true, to_apply=%region_2.0 | all-reduce | flops 32 | bytes 256 | tf_op jit(solution)/shard_map/psum | solution.py:79
  21.1 3.6 %convolution_bitcast_fusion.1 = f32[4,8,16,128]{3,1,2,0:T(8,128)S(1)} fusion(bf16[1280,2048]{1,0:T(8,128)(2,1)} %param.22, bf16[32,1280]{1,0:T(8,128)(2,1)} %param.20, f32[1280]{0:T(1024)} %param.21, f32[32]{0:T(128)S(1)} %add_rsqrt_fusion.3), kind=kOutput, calls=%fused_computation.38 | convolution fusion | flops 167936000 | bytes 5592192 | tf_op jit(solution)/shard_map/dot_general | solution.py:83
  27.3 32.1 %all-reduce.5.cloned.1.call-done = f32[32,16,128]{2,1,0:T(8,128)} async-done(((f32[32,16,128]{2,1,0:T(8,128)}), f32[32,16,128]{2,1,0:T(8,128)}) %all-reduce.5.cloned.1.call-update) | async-done | bytes 262160 | tf_op jit(solution)/shard_map/psum | solution.py:88
  62.2 12.0 %while.30 = (s32[]{:T(128)}, f32[32,2,8]{0,2,1:T(8,128)S(1)}, f32[32,2,8]{0,2,1:T(8,128)S(1)}, f32[32,2,8,128]{3,0,2,1:T(8,128)S(1)}, s32[]{:T(128)}, /*index=5*...) while((s32[]{:T(128)}, f32[32,2,8]{0,2,1:T(8,128)S(1)}, ...), condition=%wide.region_8.9_spmd.clone, body=%wide.region_5.8_spmd.clone.sunk | while | flops 274367744 | bytes 10269107 | solution.py:137
  62.3 2.0 constant_dynamic-slice_fusion.6
  66.3 1.9 constant_dynamic-slice_fusion.6
  70.3 1.9 constant_dynamic-slice_fusion.6
  75.5 39.0 %all-reduce = (bf16[32,256]{1,0:T(8,128)(2,1)S(1)}, f32[32,2,128]{2,0,1:T(8,128)S(1)}) all-reduce(f32[32,256]{1,0:T(8,128)S(1)} %fusion.45, f32[32,2,128]{2,0,1:T(8,128)S(1)} %bitcast.129), channel_id=1, replica_groups=mesh['groups'=2,'mem'=4,'head'=2,'width'=2] {'mem'}, use_global_device_ids=true, to_apply=%region_14.15 | all-reduce | flops 16384 | bytes 114688 | tf_op jit(solution)/shard_map/psum | solution.py:88
  114.9 14.1 %all-gather.1 = f32[128,2,8]{2,1,0:T(2,128)S(1)} all-gather(f32[32,2,8]{2,1,0:T(2,128)S(1)} %copy.92), channel_id=3, replica_groups=mesh['groups'=2,'mem'=4,'head'=2,'width'=2] {'mem'}, dimensions={0}, use_global_device_ids=true | all-gather | bytes 10240 | tf_op jit(solution)/shard_map/all_gather | solution.py:14
  129.0 13.3 %all-gather = f32[128,2,8]{2,1,0:T(2,128)S(1)} all-gather(f32[32,2,8]{2,1,0:T(2,128)S(1)} %copy.91), channel_id=2, replica_groups=mesh['groups'=2,'mem'=4,'head'=2,'width'=2] {'mem'}, dimensions={0}, use_global_device_ids=true | all-gather | bytes 10240 | tf_op jit(solution)/shard_map/all_gather | solution.py:14
  144.8 1.2 slice.53
  146.0 1.7 while.29
  148.8 4.1 %fusion.32 = f32[32,1280]{1,0:T(8,128)} fusion(bf16[2048,1280]{1,0:T(8,128)(2,1)} %param.31, bf16[4,8,16,128]{3,2,1,0:T(8,128)(2,1)S(1)} %bitcast.122), kind=kOutput, calls=%fused_computation.66 | convolution fusion | flops 167772160 | bytes 5537792 | tf_op jit(solution)/shard_map/dot_general | solution.py:168
  152.9 31.2 %all-reduce.7.cloned.1.call-done = f32[32,1280]{1,0:T(8,128)} async-done(((f32[32,1280]{1,0:T(8,128)}), f32[32,1280]{1,0:T(8,128)}) %all-reduce.7.cloned.1.call-update) | async-done | bytes 163856 | tf_op jit(solution)/shard_map/psum | solution.py:167
  185.1 11.7 %psum.54 = f32[32]{0:T(128)S(1)} all-reduce(f32[32]{0:T(128)S(1)} %get-tuple-element.230), channel_id=1, replica_groups=mesh['groups'=2,'mem'=4,'head'=2,'width'=2] {'mem'}, use_global_device_ids=true, to_apply=%region_18.19 | all-reduce | flops 32 | bytes 256 | tf_op jit(solution)/shard_map/psum | solution.py:172
  196.8 9.6 %fusion.37 = f32[32,6400]{1,0:T(8,128)} fusion(bf16[1280,6400]{1,0:T(8,128)(2,1)} %param.34, bf16[32,1280]{1,0:T(8,128)(2,1)S(1)} %get-tuple-element.231, f32[1280]{0:T(1024)S(1)} %copy-done.5, f32[32]{0:T(128)S(1)} %add_rsqrt_fusion.2), kind=kOutput, calls=%fused_computation.82 | convolution fusion | flops 524451840 | bytes 17290368 | tf_op jit(solution)/shard_map/dot_general | solution.py:177
  206.7 9.7 %fusion.39 = f32[32,6400]{1,0:T(8,128)} fusion(bf16[1280,6400]{1,0:T(8,128)(2,1)} %param.33, bf16[32,1280]{1,0:T(8,128)(2,1)S(1)} %get-tuple-element.231, f32[1280]{0:T(1024)S(1)} %copy-done.5, f32[32]{0:T(128)S(1)} %add_rsqrt_fusion.2), kind=kOutput, calls=%fused_computation.83 | convolution fusion | flops 524451840 | bytes 17290368 | tf_op jit(solution)/shard_map/dot_general | solution.py:176
  216.5 11.0 %reduce-scatter.5.cloned.1.call-done = f32[8,6400]{1,0:T(8,128)} async-done(((f32[32,6400]{1,0:T(8,128)}), f32[8,6400]{1,0:T(8,128)}) %reduce-scatter.5.cloned.1.call-update) | async-done | bytes 204816 | tf_op jit(solution)/shard_map/reduce_scatter | solution.py:180
  227.5 25.2 %reduce-scatter.3.cloned.1.call-done = f32[8,6400]{1,0:T(8,128)} async-done(((f32[32,6400]{1,0:T(8,128)}), f32[8,6400]{1,0:T(8,128)}) %reduce-scatter.3.cloned.1.call-update) | async-done | bytes 204816 | tf_op jit(solution)/shard_map/reduce_scatter | solution.py:179
  252.7 1.1 multiply_convert_fusion
  253.8 15.2 %all_gather.27 = bf16[32,6400]{1,0:T(8,128)(2,1)S(1)} all-gather(bf16[8,6400]{1,0:T(8,128)(2,1)S(1)} %multiply_convert_fusion), channel_id=1, replica_groups=mesh['groups'=2,'mem'=4,'head'=2,'width'=2] {'mem'}, dimensions={0}, use_global_device_ids=true | all-gather | bytes 512000 | tf_op jit(solution)/shard_map/all_gather | solution.py:182
  269.0 9.3 %fusion.52 = f32[32,1280]{1,0:T(8,128)} fusion(bf16[32,6400]{1,0:T(8,128)(2,1)S(1)} %all_gather.27, bf16[6400,1280]{1,0:T(8,128)(2,1)} %param.35), kind=kOutput, calls=%fused_computation.100 | convolution fusion | flops 524288000 | bytes 16957440 | tf_op jit(solution)/shard_map/dot_general | solution.py:186
  278.3 31.2 %all-reduce.9.cloned.1.call-done = f32[32,1280]{1,0:T(8,128)} async-done(((f32[32,1280]{1,0:T(8,128)}), f32[32,1280]{1,0:T(8,128)}) %all-reduce.9.cloned.1.call-update) | async-done | bytes 163856 | tf_op jit(solution)/shard_map/psum | solution.py:185
  309.5 1.6 fusion.31
  (132 shorter events, 19.6 us)
Async XLA Ops:
  6.5 68.4 %copy-start = (bf16[1280,256]{1,0:T(8,128)(2,1)S(1)}, bf16[1280,256]{1,0:T(8,128)(2,1)}, u32[]{:S(2)}) copy-start(bf16[1280,256]{1,0:T(8,128)(2,1)} %param.23) | copy-start | bytes 1966084
  6.5 19.0 %copy-start.6 = (s32[8192]{0:T(1024)S(1)}, s32[8192]{0:T(1024)}, u32[]{:S(2)}) copy-start(s32[8192]{0:T(1024)} %param.29) | copy-start | bytes 98308
  6.5 19.8 %copy-start.10 = (s32[16]{0:T(128)S(1)}, s32[16]{0:T(128)}, u32[]{:S(2)}) copy-start(s32[16]{0:T(128)} %param.30) | copy-start | bytes 196
  6.5 54.0 %copy-start.8 = (f32[128]{0:T(128)S(1)}, f32[128]{0:T(128)}, u32[]{:S(2)}) copy-start(f32[128]{0:T(128)} %param.25) | copy-start | bytes 1540
  6.5 52.9 %all-reduce.5.cloned.1.call-start = ((), (), s32[]{:S(2)}) async-start(), calls=%async_computation.2 | async-start | bytes 524288 | tf_op jit(solution)/shard_map/psum | solution.py:88
  25.5 118.1 %all-gather.5.cloned.1.call-start = ((), (), s32[]{:S(2)}) async-start(), calls=%async_computation.7 | async-start | bytes 1310720 | tf_op jit(solution)/shard_map/all_gather | solution.py:14
  62.1 12.8 %copy-start.2 = (bf16[32,1280]{1,0:T(8,128)(2,1)S(1)}, bf16[32,1280]{1,0:T(8,128)(2,1)}, u32[]{:S(2)}) copy-start(bf16[32,1280]{1,0:T(8,128)(2,1)} %param.20) | copy-start | bytes 245764
  62.1 12.8 %copy-start.7 = (f32[1280]{0:T(1024)S(1)}, f32[1280]{0:T(1024)}, u32[]{:S(2)}) copy-start(f32[1280]{0:T(1024)} %param.21) | copy-start | bytes 15364
  62.1 13.1 %copy-start.4 = (bf16[1280,256]{1,0:T(8,128)(2,1)S(1)}, bf16[1280,256]{1,0:T(8,128)(2,1)}, u32[]{:S(2)}) copy-start(bf16[1280,256]{1,0:T(8,128)(2,1)} %param.24) | copy-start | bytes 1966084
  62.2 52.4 %copy-start.9 = (f32[128]{0:T(128)S(1)}, f32[128]{0:T(128)}, u32[]{:S(2)}) copy-start(f32[128]{0:T(128)} %param.26) | copy-start | bytes 1540
  74.1 0.7 copy-start.3
  74.9 109.2 %all-reduce.7.cloned.1.call-start = ((), (), s32[]{:S(2)}) async-start(), calls=%async_computation.3 | async-start | bytes 327680 | tf_op jit(solution)/shard_map/psum | solution.py:167
  147.6 49.2 %copy-start.5 = (f32[1280]{0:T(1024)S(1)}, f32[1280]{0:T(1024)}, u32[]{:S(2)}) copy-start(f32[1280]{0:T(1024)} %param.32) | copy-start | bytes 15364
  152.9 74.6 %reduce-scatter.5.cloned.1.call-start = ((), (), s32[]{:S(2)}) async-start(), calls=%async_computation.5 | async-start | bytes 1024000 | tf_op jit(solution)/shard_map/reduce_scatter | solution.py:180
  206.4 46.3 %reduce-scatter.3.cloned.1.call-start = ((), (), s32[]{:S(2)}) async-start(), calls=%async_computation.4 | async-start | bytes 1024000 | tf_op jit(solution)/shard_map/reduce_scatter | solution.py:179
  216.4 93.1 %all-reduce.9.cloned.1.call-start = ((), (), s32[]{:S(2)}) async-start(), calls=%async_computation.6 | async-start | bytes 327680 | tf_op jit(solution)/shard_map/psum | solution.py:185
  269.0 42.1 %copy-start.1 = (bf16[1280,256]{1,0:T(8,128)(2,1)S(1)}, bf16[1280,256]{1,0:T(8,128)(2,1)}, u32[]{:S(2)}) copy-start(bf16[1280,256]{1,0:T(8,128)(2,1)} %param.23) | copy-start | bytes 1966084
Sparse Core Ops, SparseCore 0:
  25.6 33.7 all-reduce.4
  75.0 50.2 all-gather.4
  153.0 31.0 all-reduce.6
  206.6 20.8 reduce-scatter.4
  229.6 22.9 reduce-scatter.2
  278.4 31.0 all-reduce.8
where the time goes:
time: 319 us; the launch traced here: 318 us
  waiting for transfers between devices  131 us (41%)
  blocking collectives  107 us (34%)
  matrix products  41.5 us (13%)
  between operations  14.6 us (5%)
  other arithmetic  12 us (4%)
  local copies, waits for them, and re-layouts  11.5 us (4%)
    psum x1, blocking collectives, per_device(): lax.psum((query_part, key_part, value_part), 'mem')  39 us
    psum x1, waiting for transfers between devices, per_device(): lax.psum((query_part, key_part, value_part), 'mem')  32.1 us
    psum x1, waiting for transfers between devices, per_device(): lax.psum(jnp.dot(activated, down_weight, preferred_element_type=jnp.float...  31.2 us
    psum x1, waiting for transfers between devices, per_device(): lax.psum(jnp.dot(attended, output_weight, preferred_element_type=jnp.floa...  31.2 us
    all_gather x2, blocking collectives, combined_all(): pieces = jax.tree.map(lambda part: lax.all_gather(part, axis), value)  27.4 us
    reduce_scatter x1, waiting for transfers between devices, per_device(): lax.psum_scatter(gate_part, 'mem', scatter_dimension=0, tiled=True)  25.2 us
    all_gather x1, blocking collectives, per_device(): lax.all_gather((jax.nn.silu(gate_sum) * up_sum).astype(jnp.bfloat16), 'me...  15.2 us
    psum x1, blocking collectives, per_device(): squares = lax.psum(jnp.sum(residual * residual, axis=1), 'mem')  13.5 us
  transfers between devices with their start and end apart: 6, of which 5 were waited for; matrix products, arithmetic and copies ran while one was open for 4% of the time, Pallas kernels for 0%

commit v1 on v0

--- a/solution.py
+++ b/solution.py
@@ -182,9 +182,9 @@
     activated = lax.all_gather(
         (jax.nn.silu(gate_sum) * up_sum).astype(jnp.bfloat16), "mem", axis=0, tiled=True
     )
-    down_sum = lax.psum(
-        jnp.dot(activated, down_weight, preferred_element_type=jnp.float32), ("head", "width")
-    )
+    block = jnp.dot(activated, down_weight, preferred_element_type=jnp.float32)
+    parts = lax.all_gather(block, ("head", "width"))
+    down_sum = jnp.sum(parts, axis=0)
     return (middle_wide + down_sum).astype(jnp.bfloat16)
 
 

time: 319 us -> 293 us (0.918)
  waiting for transfers between devices: 131 us -> 99.6 us
  blocking collectives: 107 us -> 115 us
    psum x1 -> x0, waiting for transfers between devices: 31.2 us -> none  [per_device(): lax.psum(jnp.dot(activated, down_weight, preferred_element_type=jnp.float...]
    all_gather x0 -> x1, blocking collectives: none -> 7.85 us  [per_device(): parts = lax.all_gather(block, ('head', 'width'))]
  transfers between devices with their start and end apart: 6 -> 5, of which waited for: 5 -> 4; matrix products, arithmetic and copies ran while one was open for 4% -> 4% of each run, Pallas kernels for 0% -> 0%
where the time goes in v1:
time: 293 us
  blocking collectives  115 us (39%)
  waiting for transfers between devices  99.6 us (34%)
  matrix products  40.8 us (14%)
  between operations  14.2 us (5%)
  local copies, waits for them, and re-layouts  11.5 us (4%)
  other arithmetic  11.2 us (4%)
    psum x1, blocking collectives, per_device(): lax.psum((query_part, key_part, value_part), 'mem')  39 us
    psum x1, waiting for transfers between devices, per_device(): lax.psum((query_part, key_part, value_part), 'mem')  32.1 us
    psum x1, waiting for transfers between devices, per_device(): lax.psum(jnp.dot(attended, output_weight, preferred_element_type=jnp.floa...  31.2 us
    all_gather x2, blocking collectives, combined_all(): pieces = jax.tree.map(lambda part: lax.all_gather(part, axis), value)  27.4 us
    reduce_scatter x1, waiting for transfers between devices, per_device(): lax.psum_scatter(gate_part, 'mem', scatter_dimension=0, tiled=True)  25.2 us
    all_gather x1, blocking collectives, per_device(): lax.all_gather((jax.nn.silu(gate_sum) * up_sum).astype(jnp.bfloat16), 'me...  15.2 us
    psum x1, blocking collectives, per_device(): squares = lax.psum(jnp.sum(residual * residual, axis=1), 'mem')  13.5 us
    psum x1, blocking collectives, per_device(): squares_mid = lax.psum(jnp.sum(middle_wide * middle_wide, axis=1), 'mem')  11.7 us
  transfers between devices with their start and end apart: 5, of which 4 were waited for; matrix products, arithmetic and copies ran while one was open for 4% of the time, Pallas kernels for 0%

profile of v1, /device:TPU:0, one launch (start us, length us, event | category | flops | bytes accessed | tf_op | source)
XLA Modules:
  0.0 292.7 jit_solution(11246626496092515100)
XLA Ops:
  7.7 13.5 %psum.42 = f32[32]{0:T(128)S(1)} all-reduce(f32[32]{0:T(128)S(1)} %fusion.24), channel_id=1, replica_groups=mesh['groups'=2,'mem'=4,'head'=2,'width'=2] {'mem'}, use_global_device_ids=true, to_apply=%region_2.0 | all-reduce | flops 32 | bytes 256 | tf_op jit(solution)/shard_map/psum | solution.py:79
  21.1 3.6 %convolution_bitcast_fusion.1 = f32[4,8,16,128]{3,1,2,0:T(8,128)S(1)} fusion(bf16[1280,2048]{1,0:T(8,128)(2,1)} %param.22, bf16[32,1280]{1,0:T(8,128)(2,1)} %param.20, f32[1280]{0:T(1024)} %param.21, f32[32]{0:T(128)S(1)} %add_rsqrt_fusion.3), kind=kOutput, calls=%fused_computation.38 | convolution fusion | flops 167936000 | bytes 5592192 | tf_op jit(solution)/shard_map/dot_general | solution.py:83
  27.3 32.1 %all-reduce.4.cloned.1.call-done = f32[32,16,128]{2,1,0:T(8,128)} async-done(((f32[32,16,128]{2,1,0:T(8,128)}), f32[32,16,128]{2,1,0:T(8,128)}) %all-reduce.4.cloned.1.call-update) | async-done | bytes 262160 | tf_op jit(solution)/shard_map/psum | solution.py:88
  59.5 1.1 multiply_reduce_fusion
  62.2 12.0 %while.30 = (s32[]{:T(128)}, f32[32,2,8]{0,2,1:T(8,128)S(1)}, f32[32,2,8]{0,2,1:T(8,128)S(1)}, f32[32,2,8,128]{3,0,2,1:T(8,128)S(1)}, s32[]{:T(128)}, /*index=5*...) while((s32[]{:T(128)}, f32[32,2,8]{0,2,1:T(8,128)S(1)}, ...), condition=%wide.region_8.9_spmd.clone, body=%wide.region_5.8_spmd.clone.sunk | while | flops 274367744 | bytes 10269107 | solution.py:137
  62.3 2.0 constant_dynamic-slice_fusion.6
  66.3 1.9 constant_dynamic-slice_fusion.6
  70.3 1.9 constant_dynamic-slice_fusion.6
  75.5 39.0 %all-reduce = (bf16[32,256]{1,0:T(8,128)(2,1)S(1)}, f32[32,2,128]{2,0,1:T(8,128)S(1)}) all-reduce(f32[32,256]{1,0:T(8,128)S(1)} %fusion.45, f32[32,2,128]{2,0,1:T(8,128)S(1)} %bitcast.131), channel_id=1, replica_groups=mesh['groups'=2,'mem'=4,'head'=2,'width'=2] {'mem'}, use_global_device_ids=true, to_apply=%region_14.15 | all-reduce | flops 16384 | bytes 114688 | tf_op jit(solution)/shard_map/psum | solution.py:88
  114.9 14.1 %all-gather.1 = f32[128,2,8]{2,1,0:T(2,128)S(1)} all-gather(f32[32,2,8]{2,1,0:T(2,128)S(1)} %copy.92), channel_id=3, replica_groups=mesh['groups'=2,'mem'=4,'head'=2,'width'=2] {'mem'}, dimensions={0}, use_global_device_ids=true | all-gather | bytes 10240 | tf_op jit(solution)/shard_map/all_gather | solution.py:14
  129.0 13.3 %all-gather = f32[128,2,8]{2,1,0:T(2,128)S(1)} all-gather(f32[32,2,8]{2,1,0:T(2,128)S(1)} %copy.91), channel_id=2, replica_groups=mesh['groups'=2,'mem'=4,'head'=2,'width'=2] {'mem'}, dimensions={0}, use_global_device_ids=true | all-gather | bytes 10240 | tf_op jit(solution)/shard_map/all_gather | solution.py:14
  144.8 1.2 slice.53
  146.0 1.7 while.29
  148.8 4.1 %fusion.32 = f32[32,1280]{1,0:T(8,128)} fusion(bf16[2048,1280]{1,0:T(8,128)(2,1)} %param.31, bf16[4,8,16,128]{3,2,1,0:T(8,128)(2,1)S(1)} %bitcast.124), kind=kOutput, calls=%fused_computation.66 | convolution fusion | flops 167772160 | bytes 5537792 | tf_op jit(solution)/shard_map/dot_general | solution.py:168
  152.9 31.2 %all-reduce.6.cloned.1.call-done = f32[32,1280]{1,0:T(8,128)} async-done(((f32[32,1280]{1,0:T(8,128)}), f32[32,1280]{1,0:T(8,128)}) %all-reduce.6.cloned.1.call-update) | async-done | bytes 163856 | tf_op jit(solution)/shard_map/psum | solution.py:167
  185.1 11.7 %psum.47 = f32[32]{0:T(128)S(1)} all-reduce(f32[32]{0:T(128)S(1)} %get-tuple-element.230), channel_id=1, replica_groups=mesh['groups'=2,'mem'=4,'head'=2,'width'=2] {'mem'}, use_global_device_ids=true, to_apply=%region_18.19 | all-reduce | flops 32 | bytes 256 | tf_op jit(solution)/shard_map/psum | solution.py:172
  196.8 9.6 %fusion.37 = f32[32,6400]{1,0:T(8,128)} fusion(bf16[1280,6400]{1,0:T(8,128)(2,1)} %param.34, bf16[32,1280]{1,0:T(8,128)(2,1)S(1)} %get-tuple-element.231, f32[1280]{0:T(1024)S(1)} %copy-done.5, f32[32]{0:T(128)S(1)} %add_rsqrt_fusion.2), kind=kOutput, calls=%fused_computation.82 | convolution fusion | flops 524451840 | bytes 17290368 | tf_op jit(solution)/shard_map/dot_general | solution.py:177
  206.7 9.7 %fusion.39 = f32[32,6400]{1,0:T(8,128)} fusion(bf16[1280,6400]{1,0:T(8,128)(2,1)} %param.33, bf16[32,1280]{1,0:T(8,128)(2,1)S(1)} %get-tuple-element.231, f32[1280]{0:T(1024)S(1)} %copy-done.5, f32[32]{0:T(128)S(1)} %add_rsqrt_fusion.2), kind=kOutput, calls=%fused_computation.83 | convolution fusion | flops 524451840 | bytes 17290368 | tf_op jit(solution)/shard_map/dot_general | solution.py:176
  216.4 11.1 %reduce-scatter.5.cloned.1.call-done = f32[8,6400]{1,0:T(8,128)} async-done(((f32[32,6400]{1,0:T(8,128)}), f32[8,6400]{1,0:T(8,128)}) %reduce-scatter.5.cloned.1.call-update) | async-done | bytes 204816 | tf_op jit(solution)/shard_map/reduce_scatter | solution.py:180
  227.5 25.2 %reduce-scatter.3.cloned.1.call-done = f32[8,6400]{1,0:T(8,128)} async-done(((f32[32,6400]{1,0:T(8,128)}), f32[8,6400]{1,0:T(8,128)}) %reduce-scatter.3.cloned.1.call-update) | async-done | bytes 204816 | tf_op jit(solution)/shard_map/reduce_scatter | solution.py:179
  252.7 1.1 multiply_convert_fusion
  253.8 15.2 %all_gather.33 = bf16[32,6400]{1,0:T(8,128)(2,1)S(1)} all-gather(bf16[8,6400]{1,0:T(8,128)(2,1)S(1)} %multiply_convert_fusion), channel_id=1, replica_groups=mesh['groups'=2,'mem'=4,'head'=2,'width'=2] {'mem'}, dimensions={0}, use_global_device_ids=true | all-gather | bytes 512000 | tf_op jit(solution)/shard_map/all_gather | solution.py:182
  269.0 8.6 %fusion.52 = f32[32,1280]{1,0:T(8,128)S(1)} fusion(bf16[32,6400]{1,0:T(8,128)(2,1)S(1)} %all_gather.33, bf16[6400,1280]{1,0:T(8,128)(2,1)} %param.35), kind=kOutput, calls=%fused_computation.100 | convolution fusion | flops 524288000 | bytes 16957440 | tf_op jit(solution)/shard_map/dot_general | solution.py:185
  277.6 7.9 %all-gather.3 = f32[128,1280]{1,0:T(8,128)S(1)} all-gather(f32[32,1280]{1,0:T(8,128)S(1)} %fusion.52), channel_id=5, replica_groups=mesh['groups'=2,'mem'=4,'head'=2,'width'=2] {'head','width'}, dimensions={0}, use_global_device_ids=true | all-gather | bytes 819200 | tf_op jit(solution)/shard_map/all_gather | solution.py:186
  (131 shorter events, 19.1 us)
Async XLA Ops:
  6.5 68.4 %copy-start = (bf16[1280,256]{1,0:T(8,128)(2,1)S(1)}, bf16[1280,256]{1,0:T(8,128)(2,1)}, u32[]{:S(2)}) copy-start(bf16[1280,256]{1,0:T(8,128)(2,1)} %param.23) | copy-start | bytes 1966084
  6.5 19.0 %copy-start.6 = (s32[8192]{0:T(1024)S(1)}, s32[8192]{0:T(1024)}, u32[]{:S(2)}) copy-start(s32[8192]{0:T(1024)} %param.29) | copy-start | bytes 98308
  6.5 19.8 %copy-start.10 = (s32[16]{0:T(128)S(1)}, s32[16]{0:T(128)}, u32[]{:S(2)}) copy-start(s32[16]{0:T(128)} %param.30) | copy-start | bytes 196
  6.5 54.0 %copy-start.8 = (f32[128]{0:T(128)S(1)}, f32[128]{0:T(128)}, u32[]{:S(2)}) copy-start(f32[128]{0:T(128)} %param.25) | copy-start | bytes 1540
  6.5 52.9 %all-reduce.4.cloned.1.call-start = ((), (), s32[]{:S(2)}) async-start(), calls=%async_computation.2 | async-start | bytes 524288 | tf_op jit(solution)/shard_map/psum | solution.py:88
  25.5 118.1 %all-gather.6.cloned.1.call-start = ((), (), s32[]{:S(2)}) async-start(), calls=%async_computation.6 | async-start | bytes 1310720 | tf_op jit(solution)/shard_map/all_gather | solution.py:14
  62.1 12.8 %copy-start.2 = (bf16[32,1280]{1,0:T(8,128)(2,1)S(1)}, bf16[32,1280]{1,0:T(8,128)(2,1)}, u32[]{:S(2)}) copy-start(bf16[32,1280]{1,0:T(8,128)(2,1)} %param.20) | copy-start | bytes 245764
  62.1 12.8 %copy-start.7 = (f32[1280]{0:T(1024)S(1)}, f32[1280]{0:T(1024)}, u32[]{:S(2)}) copy-start(f32[1280]{0:T(1024)} %param.21) | copy-start | bytes 15364
  62.1 13.1 %copy-start.4 = (bf16[1280,256]{1,0:T(8,128)(2,1)S(1)}, bf16[1280,256]{1,0:T(8,128)(2,1)}, u32[]{:S(2)}) copy-start(bf16[1280,256]{1,0:T(8,128)(2,1)} %param.24) | copy-start | bytes 1966084
  62.2 52.4 %copy-start.9 = (f32[128]{0:T(128)S(1)}, f32[128]{0:T(128)}, u32[]{:S(2)}) copy-start(f32[128]{0:T(128)} %param.26) | copy-start | bytes 1540
  74.1 0.7 copy-start.3
  74.9 109.2 %all-reduce.6.cloned.1.call-start = ((), (), s32[]{:S(2)}) async-start(), calls=%async_computation.3 | async-start | bytes 327680 | tf_op jit(solution)/shard_map/psum | solution.py:167
  147.6 49.2 %copy-start.5 = (f32[1280]{0:T(1024)S(1)}, f32[1280]{0:T(1024)}, u32[]{:S(2)}) copy-start(f32[1280]{0:T(1024)} %param.32) | copy-start | bytes 15364
  152.9 74.6 %reduce-scatter.5.cloned.1.call-start = ((), (), s32[]{:S(2)}) async-start(), calls=%async_computation.5 | async-start | bytes 1024000 | tf_op jit(solution)/shard_map/reduce_scatter | solution.py:180
  206.4 46.3 %reduce-scatter.3.cloned.1.call-start = ((), (), s32[]{:S(2)}) async-start(), calls=%async_computation.4 | async-start | bytes 1024000 | tf_op jit(solution)/shard_map/reduce_scatter | solution.py:179
  269.0 17.2 %copy-start.1 = (bf16[1280,256]{1,0:T(8,128)(2,1)S(1)}, bf16[1280,256]{1,0:T(8,128)(2,1)}, u32[]{:S(2)}) copy-start(bf16[1280,256]{1,0:T(8,128)(2,1)} %param.23) | copy-start | bytes 1966084
Sparse Core Ops, SparseCore 0:
  25.6 33.7 all-reduce.3
  75.0 50.2 all-gather.5
  153.0 31.0 all-reduce.5
  206.6 20.8 reduce-scatter.4
  229.6 22.9 reduce-scatter.2
